TPU v7x, 32 devices: a whole 2x2x4 slice. The times are simulated.
32 devices in a mesh: section: 2 (over core), group: 4 (over y, x), dp: 4 (over z).
Axes of the slice: x: 2, y: 2, z: 4, core: 2. Of those that a mesh axis runs over, the one named last changes fastest.
Arguments:
- tokens: bfloat16 [2, 4096, 768], P(None, ('group', 'dp')), may hold values from -6 to 6
- cotangent: bfloat16 [2, 4096, 768], P(None, ('group', 'dp')), may hold values from -6 to 6
- lengths: int32 [2, 16, 3], P(None, ('group', 'dp')), may hold values from 1 to 128, 256 in all within a row
- attend_gain: bfloat16 [2, 768], P('section', 'dp'), may hold values from 0.5 to 1.5
- attend_bias: bfloat16 [2, 768], P('section', 'dp'), may hold values from -1.5 to 1.5
- qkv_weight: bfloat16 [2, 768, 2304], P('section', 'dp'), may hold values from -0.21875 to 0.21875
- out_weight: bfloat16 [2, 768, 768], P('section', 'dp'), may hold values from -0.875 to 0.875
- feed_gain: bfloat16 [2, 768], P('section', 'dp'), may hold values from 0.5 to 1.5
- feed_bias: bfloat16 [2, 768], P('section', 'dp'), may hold values from -1.5 to 1.5
- up_weight: bfloat16 [2, 768, 3072], P('section', 'dp'), may hold values from -0.21875 to 0.21875
- down_weight: bfloat16 [2, 3072, 768], P('section', 'dp'), may hold values from -0.109375 to 0.109375
Outputs:
- layer_out: bfloat16 [2, 2, 4096, 768], P('section', None, ('group', 'dp'))
- input_grad: bfloat16 [2, 2, 4096, 768], P('section', None, ('group', 'dp'))
- attend_gain_grad: float32 [2, 768], P('section', 'dp')
- attend_bias_grad: float32 [2, 768], P('section', 'dp')
- qkv_grad: float32 [2, 768, 2304], P('section', 'dp')
- out_grad: float32 [2, 768, 768], P('section', 'dp')
- feed_gain_grad: float32 [2, 768], P('section', 'dp')
- feed_bias_grad: float32 [2, 768], P('section', 'dp')
- up_grad: float32 [2, 768, 3072], P('section', 'dp')
- down_grad: float32 [2, 3072, 768], P('section', 'dp')
Inputs may be any that keep to these rules, and one draw needn't show every extreme that they name: The 3 lengths of one device's block of a micro-batch add up to 256; the longest sequence of every block has 128 tokens.
All inputs are finite; a program needn't handle non-finite values.
Results may differ from a plain program's by a relative error of at most 0.02.
Values may be sent and summed in bfloat16 or wider, within the bound.
No kernel may reach another device: no remote copies, remote signals or barrier semaphores. Data moves between devices by JAX's collectives and lax.ppermute only.
A program may use at most 192 MiB of HBM per device.

v0:
```python
import jax
import jax.numpy as jnp
from jax import lax
from jax.sharding import PartitionSpec as P

HEAD_DIM = 64
masked_score = -1000000000.0


def from_behind(block, axis, distance):
    devices = range(lax.axis_size(axis))
    route = [(i - distance, i) for i in devices if i - distance in devices]
    return lax.ppermute(block, axis, route)


def rope_tables(lengths_row, tok):
    bounds = jnp.cumsum(lengths_row, dtype=jnp.int32)
    places = jnp.arange(tok, dtype=jnp.int32)
    segment = jnp.sum((places[:, None] >= bounds[None, :-1]).astype(jnp.int32), axis=1)
    starts = bounds - lengths_row
    picks = jnp.arange(lengths_row.shape[0], dtype=jnp.int32)
    begin = jnp.sum(jnp.where(segment[:, None] == picks[None, :], starts[None, :], 0), axis=1)
    offset = (places - begin).astype(jnp.float32)
    half = HEAD_DIM // 2
    freqs = 10000.0 ** (-jnp.arange(half, dtype=jnp.float32) / half)
    angles = offset[:, None] * freqs[None, :]
    return (jnp.cos(angles), jnp.sin(angles), segment[:, None] == segment[None, :])


def layer_norm(x, gain, bias):
    center = x - jnp.mean(x, axis=-1, keepdims=True)
    spread = jnp.mean(center * center, axis=-1, keepdims=True)
    return center * lax.rsqrt(spread + 1e-05) * gain + bias


def rotate(heads_in, cosine, sine):
    half = heads_in.shape[-1] // 2
    first = heads_in[..., :half]
    second = heads_in[..., half:]
    cosv = cosine[:, None, :]
    sinv = sine[:, None, :]
    return jnp.concatenate([first * cosv - second * sinv, second * cosv + first * sinv], axis=-1)


def inner(left, right):
    return lax.dot_general(
        left, right, (((0,), (0,)), ((), ())), preferred_element_type=jnp.float32
    )


def times_transposed(left, weight):
    return lax.dot_general(
        left, weight, (((1,), (1,)), ((), ())), preferred_element_type=jnp.float32
    )


def layer_parts(x, weights, tables):
    gain_one, bias_one, qkv_w, out_w, gain_two, bias_two, up_w, down_w = weights
    cosine, sine, same = tables
    tok, width = x.shape
    heads = width // HEAD_DIM
    normed = layer_norm(x, gain_one.astype(jnp.float32), bias_one.astype(jnp.float32)).astype(
        jnp.bfloat16
    )
    qkv = jnp.dot(normed, qkv_w, preferred_element_type=jnp.float32).reshape(
        tok, 3, heads, HEAD_DIM
    )
    query = rotate(qkv[:, 0], cosine, sine).astype(jnp.bfloat16)
    key = rotate(qkv[:, 1], cosine, sine).astype(jnp.bfloat16)
    value = qkv[:, 2].astype(jnp.bfloat16)
    scores = jnp.einsum(
        "qhd,khd->hqk", query, key, preferred_element_type=jnp.float32
    ) * HEAD_DIM ** (-0.5)
    scores = jnp.where(same[None], scores, masked_score)
    peak = jnp.max(scores, axis=-1, keepdims=True)
    expd = jnp.exp(scores - peak)
    probs = expd / jnp.sum(expd, axis=-1, keepdims=True)
    probs_low = probs.astype(jnp.bfloat16)
    mixed = jnp.einsum("hqk,khd->qhd", probs_low, value, preferred_element_type=jnp.float32)
    mixed = mixed.reshape(tok, width).astype(jnp.bfloat16)
    resid = x + jnp.dot(mixed, out_w, preferred_element_type=jnp.float32)
    normed_two = layer_norm(
        resid, gain_two.astype(jnp.float32), bias_two.astype(jnp.float32)
    ).astype(jnp.bfloat16)
    upward = jnp.dot(normed_two, up_w, preferred_element_type=jnp.float32)
    active = jax.nn.gelu(upward, approximate=False).astype(jnp.bfloat16)
    return (normed, query, key, value, probs, probs_low, mixed, resid, normed_two, upward, active)


def layer_forward(x, weights, tables):
    saved = layer_parts(x, weights, tables)
    return saved[7] + jnp.dot(saved[10], weights[7], preferred_element_type=jnp.float32)


def layer_backward(x, upstream, weights, tables):
    gain_one, bias_one, qkv_w, out_w, gain_two, bias_two, up_w, down_w = weights
    cosine, sine, same = tables
    normed, query, key, value, probs, probs_low, mixed, resid, normed_two, upward, active = (
        layer_parts(x, weights, tables)
    )
    tok, width = x.shape
    heads = width // HEAD_DIM
    scale = HEAD_DIM ** (-0.5)
    d_branch_ff = upstream.astype(jnp.bfloat16)
    g_down = inner(active, d_branch_ff)
    d_active = times_transposed(d_branch_ff, down_w)
    _, gelu_pull = jax.vjp(lambda u: jax.nn.gelu(u, approximate=False), upward)
    d_up = gelu_pull(d_active)[0].astype(jnp.bfloat16)
    g_up = inner(normed_two, d_up)
    d_normed_two = times_transposed(d_up, up_w)
    _, norm_pull_two = jax.vjp(
        layer_norm, resid, gain_two.astype(jnp.float32), bias_two.astype(jnp.float32)
    )
    d_resid_part, g_gain_two, g_bias_two = norm_pull_two(d_normed_two)
    d_resid = upstream + d_resid_part
    d_branch = d_resid.astype(jnp.bfloat16)
    g_out = inner(mixed, d_branch)
    d_mixed = times_transposed(d_branch, out_w).astype(jnp.bfloat16).reshape(tok, heads, HEAD_DIM)
    d_value = jnp.einsum("hqk,qhd->khd", probs_low, d_mixed, preferred_element_type=jnp.float32)
    d_probs = jnp.einsum("qhd,khd->hqk", d_mixed, value, preferred_element_type=jnp.float32)
    d_scores = probs * (d_probs - jnp.sum(d_probs * probs, axis=-1, keepdims=True))
    d_scores = d_scores.astype(jnp.bfloat16)
    d_query = jnp.einsum("hqk,khd->qhd", d_scores, key, preferred_element_type=jnp.float32) * scale
    d_key = jnp.einsum("hqk,qhd->khd", d_scores, query, preferred_element_type=jnp.float32) * scale
    d_qkv = jnp.stack(
        [rotate(d_query, cosine, -sine), rotate(d_key, cosine, -sine), d_value], axis=1
    )
    d_qkv = d_qkv.reshape(tok, 3 * width).astype(jnp.bfloat16)
    g_qkv = inner(normed, d_qkv)
    d_normed = times_transposed(d_qkv, qkv_w)
    _, norm_pull_one = jax.vjp(
        layer_norm, x, gain_one.astype(jnp.float32), bias_one.astype(jnp.float32)
    )
    d_x_part, g_gain_one, g_bias_one = norm_pull_one(d_normed)
    d_x = d_resid + d_x_part
    return (d_x, (g_gain_one, g_bias_one, g_qkv, g_out, g_gain_two, g_bias_two, g_up, g_down))


def pick_tables(first, early, late):
    return tuple((jnp.where(first, a, b) for a, b in zip(early, late)))


def on_device(
    tokens,
    cotangent,
    lengths,
    attend_gain,
    attend_bias,
    qkv_weight,
    out_weight,
    feed_gain,
    feed_bias,
    up_weight,
    down_weight,
):
    first = lax.axis_index("section") == 0
    micro = tokens.shape[0]
    tok = tokens.shape[1]
    width = tokens.shape[2]
    shards = (
        attend_gain[0],
        attend_bias[0],
        qkv_weight[0],
        out_weight[0],
        feed_gain[0],
        feed_bias[0],
        up_weight[0],
        down_weight[0],
    )
    weights = (
        lax.all_gather(shards[0], "dp", axis=0, tiled=True),
        lax.all_gather(shards[1], "dp", axis=0, tiled=True),
        lax.all_gather(shards[2], "dp", axis=0, tiled=True),
        lax.all_gather(shards[3], "dp", axis=0, tiled=True),
        lax.all_gather(shards[4], "dp", axis=0, tiled=True),
        lax.all_gather(shards[5], "dp", axis=0, tiled=True),
        lax.all_gather(shards[6], "dp", axis=0, tiled=True),
        lax.all_gather(shards[7], "dp", axis=0, tiled=True),
    )
    tables = [rope_tables(lengths[m, 0], tok) for m in range(micro)]
    received = jnp.zeros((tok, width), jnp.bfloat16)
    inputs = []
    outputs = []
    for tick in range(micro + 1):
        mine = min(tick, micro - 1)
        theirs = max(tick - 1, 0)
        source = jnp.where(first, tokens[mine], received).astype(jnp.float32)
        tabs = pick_tables(first, tables[mine], tables[theirs])
        result = layer_forward(source, weights, tabs).astype(jnp.bfloat16)
        inputs.append(source)
        outputs.append(result)
        if tick < micro:
            received = from_behind(result, "section", 1)
    kept = [jnp.where(first, inputs[m], inputs[m + 1]) for m in range(micro)]
    layer_out = jnp.stack([jnp.where(first, outputs[m], outputs[m + 1]) for m in range(micro)])
    totals = tuple((jnp.zeros(w.shape, jnp.float32) for w in weights))
    received = jnp.zeros((tok, width), jnp.bfloat16)
    sent_back = []
    for tick in range(micro + 1):
        late = min(micro - tick, micro - 1)
        early = max(micro - 1 - tick, 0)
        valid = jnp.where(first, float(tick >= 1), float(tick < micro))
        upstream = jnp.where(first, received, cotangent[early]).astype(jnp.float32)
        source = jnp.where(first, kept[late], kept[early])
        tabs = pick_tables(first, tables[late], tables[early])
        d_x, grads = layer_backward(source, upstream, weights, tabs)
        totals = tuple((total + valid * grad for total, grad in zip(totals, grads)))
        d_low = d_x.astype(jnp.bfloat16)
        sent_back.append(d_low)
        if tick < micro:
            received = from_behind(d_low, "section", -1)
    input_grad = jnp.stack(
        [jnp.where(first, sent_back[micro - m], sent_back[micro - 1 - m]) for m in range(micro)]
    )
    rows = (
        lax.psum_scatter(
            totals[0].astype(jnp.bfloat16), "dp", scatter_dimension=0, tiled=True
        ).astype(jnp.float32),
        lax.psum_scatter(
            totals[1].astype(jnp.bfloat16), "dp", scatter_dimension=0, tiled=True
        ).astype(jnp.float32),
        lax.psum_scatter(
            totals[2].astype(jnp.bfloat16), "dp", scatter_dimension=0, tiled=True
        ).astype(jnp.float32),
        lax.psum_scatter(
            totals[3].astype(jnp.bfloat16), "dp", scatter_dimension=0, tiled=True
        ).astype(jnp.float32),
        lax.psum_scatter(
            totals[4].astype(jnp.bfloat16), "dp", scatter_dimension=0, tiled=True
        ).astype(jnp.float32),
        lax.psum_scatter(
            totals[5].astype(jnp.bfloat16), "dp", scatter_dimension=0, tiled=True
        ).astype(jnp.float32),
        lax.psum_scatter(
            totals[6].astype(jnp.bfloat16), "dp", scatter_dimension=0, tiled=True
        ).astype(jnp.float32),
        lax.psum_scatter(
            totals[7].astype(jnp.bfloat16), "dp", scatter_dimension=0, tiled=True
        ).astype(jnp.float32),
    )
    summed = (
        lax.psum(rows[0].astype(jnp.bfloat16), "group").astype(jnp.float32),
        lax.psum(rows[1].astype(jnp.bfloat16), "group").astype(jnp.float32),
        lax.psum(rows[2].astype(jnp.bfloat16), "group").astype(jnp.float32),
        lax.psum(rows[3].astype(jnp.bfloat16), "group").astype(jnp.float32),
        lax.psum(rows[4].astype(jnp.bfloat16), "group").astype(jnp.float32),
        lax.psum(rows[5].astype(jnp.bfloat16), "group").astype(jnp.float32),
        lax.psum(rows[6].astype(jnp.bfloat16), "group").astype(jnp.float32),
        lax.psum(rows[7].astype(jnp.bfloat16), "group").astype(jnp.float32),
    )
    return (
        layer_out[None],
        input_grad[None],
        summed[0][None],
        summed[1][None],
        summed[2][None],
        summed[3][None],
        summed[4][None],
        summed[5][None],
        summed[6][None],
        summed[7][None],
    )


def solution(mesh):
    placed = (
        P(None, ("group", "dp"), None),
        P(None, ("group", "dp"), None),
        P(None, ("group", "dp"), None),
        P("section", "dp"),
        P("section", "dp"),
        P("section", "dp", None),
        P("section", "dp", None),
        P("section", "dp"),
        P("section", "dp"),
        P("section", "dp", None),
        P("section", "dp", None),
    )
    return jax.shard_map(
        on_device,
        mesh=mesh,
        in_specs=placed,
        out_specs=(
            P("section", None, ("group", "dp"), None),
            P("section", None, ("group", "dp"), None),
            P("section", "dp"),
            P("section", "dp"),
            P("section", "dp", None),
            P("section", "dp", None),
            P("section", "dp"),
            P("section", "dp"),
            P("section", "dp", None),
            P("section", "dp", None),
        ),
        check_vma=False,
    )
```

profile of v0, /device:TPU:0, one launch (start us, length us, event | category | flops | bytes accessed | tf_op | source)
XLA Modules:
  0.0 874.4 jit_solution(11148271096684498808)
XLA Ops:
  12.4 13.9 %all-reduce.9 = (bf16[768]{0:T(1024)(128)(2,1)S(1)}, bf16[768]{0:T(1024)(128)(2,1)S(1)}, bf16[768]{0:T(1024)(128)(2,1)S(1)}, bf16[768]{0:T(1024)(128)(2,1)S(1)}) all-reduce(bf16[768]{0:T(1024)(128)(2,1)S(1)} %dynamic-update-slice.1, bf16[768]{0:T(1024)(128)(2,1)S(1)} %dynamic-update-slice, ...), channel_id=3, replica_groups=mesh['section'=2,'group'=4,'dp'=4] {'dp'}, use_global_device_ids=true, to_apply=%add.1 | all-reduce | flops 3072 | bytes 12288
  29.2 53.3 %all-gather.13.cloned.1.call-done = bf16[1,768,2304]{2,1,0:T(8,128)(2,1)} async-done(((bf16[1,192,2304]{2,1,0:T(8,128)(2,1)}), bf16[1,768,2304]{2,1,0:T(8,128)(2,1)}) %all-gather.13.cloned.1.call-update) | async-done | bytes 3538960 | tf_op jit(solution)/shard_map/all_gather | solution.py:173
  82.5 5.8 copy.96
  88.3 3.4 fusion.365
  94.5 18.6 %all-gather.15.cloned.1.call-done = bf16[1,768,768]{2,1,0:T(8,128)(2,1)} async-done(((bf16[1,192,768]{2,1,0:T(8,128)(2,1)}), bf16[1,768,768]{2,1,0:T(8,128)(2,1)}) %all-gather.15.cloned.1.call-update) | async-done | bytes 1179664 | tf_op jit(solution)/shard_map/all_gather | solution.py:174
  115.2 88.0 %all-gather.19.cloned.1.call-done = bf16[1,3072,768]{2,1,0:T(8,128)(2,1)} async-done(((bf16[1,768,768]{2,1,0:T(8,128)(2,1)}), bf16[1,3072,768]{2,1,0:T(8,128)(2,1)}) %all-gather.19.cloned.1.call-update) | async-done | bytes 4718608 | tf_op jit(solution)/shard_map/all_gather | solution.py:178
  203.3 89.3 %all-gather.17.cloned.1.call-done = bf16[1,768,3072]{2,1,0:T(8,128)(2,1)} async-done(((bf16[1,192,3072]{2,1,0:T(8,128)(2,1)}), bf16[1,768,3072]{2,1,0:T(8,128)(2,1)}) %all-gather.17.cloned.1.call-update) | async-done | bytes 4718608 | tf_op jit(solution)/shard_map/all_gather | solution.py:177
  292.6 12.8 %fusion.287 = bf16[256,768]{1,0:T(8,128)(2,1)S(1)} fusion(f32[256,768]{1,0:T(8,128)S(1)} %get-tuple-element.155, bf16[1,3072,768]{2,1,0:T(8,128)(2,1)} %all-gather.19.cloned.1.call-done, bf16[1,768,3072]{2,1,0:T(8,128)(2,1)} %all-gather.17.cloned.1.call-done, f32[768]{0:T(1024)S(1)} %convert_element_type.462, f32[768]{0:T(1024)S(1)} %convert_element_type.461, ...), kind=kOutput, calls=%fused_computation.351 | convolution fusion | flops 2468413440 | bytes 10625024 | tf_op jit(solution)/shard_map/dot_general | solution.py:92
  309.0 3.7 fusion.48
  317.8 12.8 %fusion.280 = bf16[256,768]{1,0:T(8,128)(2,1)S(1)} fusion(f32[256,768]{1,0:T(8,128)S(1)} %get-tuple-element.159, bf16[1,3072,768]{2,1,0:T(8,128)(2,1)} %all-gather.19.cloned.1.call-done, bf16[1,768,3072]{2,1,0:T(8,128)(2,1)} %all-gather.17.cloned.1.call-done, f32[768]{0:T(1024)S(1)} %convert_element_type.462, f32[768]{0:T(1024)S(1)} %convert_element_type.461, ...), kind=kOutput, calls=%fused_computation.350 | convolution fusion | flops 2468413440 | bytes 10625024 | tf_op jit(solution)/shard_map/dot_general | solution.py:92
  330.6 3.2 collective-permute-start.1
  341.5 4.6 fusion.606
  346.1 2.5 convolution_convert_fusion.8
  349.5 4.6 fusion.28
  354.2 9.8 %add_convert_fusion.5 = bf16[256,3072]{1,0:T(8,128)(2,1)S(1)} fusion(bf16[1,3072,768]{2,1,0:T(8,128)(2,1)S(1)} %bitcast.436, f32[256,3072]{1,0:T(8,128)S(1)} %fusion.28, bf16[2,256,768]{2,1,0:T(8,128)(2,1)S(1)} %copy-done.45, pred[]{:T(512)S(6)} %eq.69), kind=kOutput, calls=%fused_computation.112 | convolution fusion | flops 1264779264 | bytes 9830401 | tf_op jit(solution)/shard_map/dot_general | solution.py:52
  364.0 2.2 multiply_reduce_fusion.5
  371.6 2.7 fusion.294
  383.0 2.2 multiply_reduce_fusion.8
  387.9 3.1 fusion.40
  393.6 4.7 fusion.610
  398.3 2.5 convolution_convert_fusion.5
  410.0 4.6 fusion.612
  414.7 2.6 convolution_convert_fusion.2
  419.0 3.9 fusion.24
  423.1 3.1 fusion.20
  426.2 4.2 fusion.589
  431.5 9.1 %add_convert_fusion.4 = bf16[256,3072]{1,0:T(8,128)(2,1)S(1)} fusion(bf16[256,768]{1,0:T(8,128)(2,1)S(1)} %bitcast_select_fusion.1, bf16[1,3072,768]{2,1,0:T(8,128)(2,1)S(1)} %bitcast.438, f32[256,3072]{1,0:T(8,128)S(1)} %fusion.24), kind=kOutput, calls=%fused_computation.95 | convolution fusion | flops 1264582656 | bytes 9830400 | tf_op jit(solution)/shard_map/dot_general | solution.py:52
  448.1 2.7 fusion.295
  464.0 4.2 fusion.587
  468.4 9.3 %add_convert_fusion.3 = bf16[256,3072]{1,0:T(8,128)(2,1)S(1)} fusion(bf16[256,768]{1,0:T(8,128)(2,1)S(1)} %bitcast_select_fusion, bf16[1,3072,768]{2,1,0:T(8,128)(2,1)S(1)} %bitcast.440, f32[256,3072]{1,0:T(8,128)S(1)} %copy-done.180), kind=kOutput, calls=%fused_computation.78 | convolution fusion | flops 1264582656 | bytes 9830400 | tf_op jit(solution)/shard_map/dot_general | solution.py:52
  482.0 5.1 multiply_reduce_fusion
  488.9 3.5 multiply_convert_fusion.3
  498.6 3.3 add_convert_fusion.2
  503.0 3.1 fusion.586
  507.8 6.2 add_convert_fusion.1
  515.1 9.7 %fusion.127 = f32[3072,768]{1,0:T(8,128)S(1)} fusion(f32[256,3072]{1,0:T(8,128)} %copy-done.179, bf16[2,256,768]{2,1,0:T(8,128)(2,1)S(1)} %copy-done.49, pred[]{:T(512)S(6)} %eq.69), kind=kOutput, calls=%fused_computation.191 | convolution fusion | flops 1259274240 | bytes 12976129 | tf_op jit(solution)/shard_map/dot_general | solution.py:46
  524.9 9.9 %fusion.128 = f32[3072,768]{1,0:T(8,128)} fusion(bf16[256,768]{1,0:T(8,128)(2,1)S(1)} %copy-done.31, f32[256,3072]{1,0:T(8,128)S(1)} %copy-done.183), kind=kOutput, calls=%fused_computation.192 | convolution fusion | flops 1259077632 | bytes 12976128 | tf_op jit(solution)/shard_map/dot_general | solution.py:46
  534.8 11.8 %add_convert_fusion = bf16[3072,768]{1,0:T(8,128)(2,1)} fusion(f32[3072,768]{1,0:T(8,128)} %fusion.128, f32[3072,768]{1,0:T(8,128)S(1)} %fusion.127, bf16[256,768]{1,0:T(8,128)(2,1)S(1)} %copy-done.37, f32[]{:T(128)S(6)} %select_n.198, f32[]{:T(128)S(6)} %select_n.197, f32[256,3072]{1,0:T(8,128)S(1)} %copy-done.181), kind=kOutput, calls=%fused_computation.6 | convolution fusion | flops 1270874112 | bytes 27131912 | tf_op jit(solution)/shard_map/dot_general | solution.py:46
  548.5 3.7 fusion.46
  557.7 27.9 %reduce-scatter.5.cloned.1.call-done = bf16[192,2304]{1,0:T(8,128)(2,1)} async-done(((bf16[768,2304]{1,0:T(8,128)(2,1)}), bf16[192,2304]{1,0:T(8,128)(2,1)}) %reduce-scatter.5.cloned.1.call-update) | async-done | bytes 884752 | tf_op jit(solution)/shard_map/reduce_scatter | solution.py:222
  585.6 87.9 %reduce-scatter.9.cloned.1.call-done = bf16[192,3072]{1,0:T(8,128)(2,1)} async-done(((bf16[768,3072]{1,0:T(8,128)(2,1)}), bf16[192,3072]{1,0:T(8,128)(2,1)}) %reduce-scatter.9.cloned.1.call-update) | async-done | bytes 1179664 | tf_op jit(solution)/shard_map/reduce_scatter | solution.py:234
  673.5 88.1 %reduce-scatter.11.cloned.1.call-done = bf16[768,768]{1,0:T(8,128)(2,1)} async-done(((bf16[3072,768]{1,0:T(8,128)(2,1)}), bf16[768,768]{1,0:T(8,128)(2,1)}) %reduce-scatter.11.cloned.1.call-update) | async-done | bytes 1179664 | tf_op jit(solution)/shard_map/reduce_scatter | solution.py:237
  761.7 13.7 %fusion.314 = bf16[1,256,768]{2,1,0:T(8,128)(2,1)} fusion(bf16[256,768]{1,0:T(8,128)(2,1)} %copy-done.88, f32[256,768]{1,0:T(8,128)S(1)} %copy-done.40, bf16[1,3072,768]{2,1,0:T(8,128)(2,1)} %all-gather.19.cloned.1.call-done, bf16[1,768,3072]{2,1,0:T(8,128)(2,1)} %all-gather.17.cloned.1.call-done, f32[768]{0:T(1024)S(1)} %convert_element_type.462, ...), kind=kOutput, calls=%fused_computation.378 | convolution fusion | flops 2468610048 | bytes 11018241 | tf_op jit(solution)/shard_map/dot_general | solution.py:92
  777.5 4.8 multiply_reduce_fusion.6
  782.4 11.1 %all-reduce.8 = (bf16[768]{0:T(1024)(128)(2,1)S(1)}, bf16[768]{0:T(1024)(128)(2,1)S(1)}, bf16[768]{0:T(1024)(128)(2,1)S(1)}, bf16[768]{0:T(1024)(128)(2,1)S(1)}) all-reduce(bf16[768]{0:T(1024)(128)(2,1)S(1)} %add_convert_fusion.46, ...), channel_id=10, replica_groups=mesh['section'=2,'group'=4,'dp'=4] {'dp'}, use_global_device_ids=true, to_apply=%region_60.61.clone | all-reduce | flops 3072 | bytes 12288
  793.8 10.2 %all-reduce.10 = (bf16[1,192]{1,0:T(2,128)(2,1)S(1)}, bf16[1,192]{1,0:T(2,128)(2,1)S(1)}, bf16[1,192]{1,0:T(2,128)(2,1)S(1)}, bf16[1,192]{1,0:T(2,128)(2,1)S(1)}) all-reduce(bf16[1,192]{1,0:T(2,128)(2,1)S(1)} %broadcast_in_dim.143, ...), channel_id=1, replica_groups=mesh['section'=2,'group'=4,'dp'=4] {'group'}, use_global_device_ids=true, to_apply=%region_61.62 | all-reduce | flops 768 | bytes 3072 | tf_op jit(solution)/shard_map/psum | solution.py:242
  809.8 50.1 %all-reduce.14.cloned.1.call-done = (bf16[1,192,2304]{2,1,0:T(8,128)(2,1)}, bf16[1,192,768]{2,1,0:T(8,128)(2,1)}, bf16[1,192,3072]{2,1,0:T(8,128)(2,1)}, bf16[1,768,768]{2,1,0:T(8,128)(2,1)}) async-done(((bf16[1,192,2304]{2,1,0:T(8,128)(2,1)}, bf16[1,192,768]{2,1,0:T(8,128)(2,1)}, bf16[1,192,3072]{2,1,0:T(8,128)(2,1)}, bf16[1,768,768]{2,1,0:T(8,128)(2,1)}), (bf16[1,192,2304]{2,1,0:T(8,128)(2,1)}, ...) | async-done | bytes 3538960 | tf_op jit(solution)/shard_map/psum | solution.py:244
  860.0 2.6 broadcast_in_dim.148
  (616 shorter events, 115.8 us)
Async XLA Ops:
  7.2 19.1 %copy-start.157 = (s32[2,1,3]{2,1,0:T(1,128)S(1)}, s32[2,1,3]{2,1,0:T(1,128)}, u32[]{:S(2)}) copy-start(s32[2,1,3]{2,1,0:T(1,128)} %param.13) | copy-start | bytes 76
  7.2 19.7 %copy-start.7 = (bf16[2,256,768]{2,1,0:T(8,128)(2,1)S(1)}, bf16[2,256,768]{2,1,0:T(8,128)(2,1)}, u32[]{:S(2)}) copy-start(bf16[2,256,768]{2,1,0:T(8,128)(2,1)} %param.11) | copy-start | bytes 2359300
  7.3 75.3 %all-gather.13.cloned.1.call-start = ((), (), s32[]{:S(2)}) async-start(), calls=%async_computation.8 | async-start | bytes 4423680 | tf_op jit(solution)/shard_map/all_gather | solution.py:173
  8.0 105.1 %all-gather.15.cloned.1.call-start = ((), (), s32[]{:S(2)}) async-start(), calls=%async_computation.9 | async-start | bytes 1474560 | tf_op jit(solution)/shard_map/all_gather | solution.py:174
  8.7 194.5 %all-gather.19.cloned.1.call-start = ((), (), s32[]{:S(2)}) async-start(), calls=%async_computation.11 | async-start | bytes 5898240 | tf_op jit(solution)/shard_map/all_gather | solution.py:178
  9.5 283.1 %all-gather.17.cloned.1.call-start = ((), (), s32[]{:S(2)}) async-start(), calls=%async_computation.10 | async-start | bytes 5898240 | tf_op jit(solution)/shard_map/all_gather | solution.py:177
  10.0 547.7 %reduce-scatter.7.cloned.1.call-start = ((), (), s32[]{:S(2)}) async-start(), calls=%async_computation.5 | async-start | bytes 1474560 | tf_op jit(solution)/shard_map/reduce_scatter | solution.py:225
  28.2 64.5 %copy-start.107 = (pred[256,256]{0,1:T(8,128)(4,1)}, pred[256,256]{0,1:T(8,128)(4,1)S(1)}, u32[]{:S(2)}) copy-start(pred[256,256]{0,1:T(8,128)(4,1)S(1)} %get-tuple-element.145) | copy-start | bytes 196612
  28.2 285.5 %copy-start.108 = (pred[256,256]{0,1:T(8,128)(4,1)}, pred[256,256]{0,1:T(8,128)(4,1)S(1)}, u32[]{:S(2)}) copy-start(pred[256,256]{0,1:T(8,128)(4,1)S(1)} %get-tuple-element.144) | copy-start | bytes 196612
  29.2 62.6 %copy-start.78 = (f32[256,32]{0,1:T(8,128)}, f32[256,32]{0,1:T(8,128)S(1)}, u32[]{:S(2)}) copy-start(f32[256,32]{0,1:T(8,128)S(1)} %get-tuple-element.141) | copy-start | bytes 98308
  29.2 62.6 %copy-start.94 = (f32[256,32]{0,1:T(8,128)}, f32[256,32]{0,1:T(8,128)S(1)}, u32[]{:S(2)}) copy-start(f32[256,32]{0,1:T(8,128)S(1)} %get-tuple-element.140) | copy-start | bytes 98308
  29.2 283.6 %copy-start.81 = (f32[256,32]{0,1:T(8,128)}, f32[256,32]{0,1:T(8,128)S(1)}, u32[]{:S(2)}) copy-start(f32[256,32]{0,1:T(8,128)S(1)} %get-tuple-element.135) | copy-start | bytes 98308
  29.2 283.6 %copy-start.96 = (f32[256,32]{0,1:T(8,128)}, f32[256,32]{0,1:T(8,128)S(1)}, u32[]{:S(2)}) copy-start(f32[256,32]{0,1:T(8,128)S(1)} %get-tuple-element.136) | copy-start | bytes 98308
  305.4 3.2 collective-permute-start
  330.6 3.8 collective-permute-start.1
  335.3 91.0 %copy-start.5 = (bf16[256,768]{1,0:T(8,128)(2,1)}, bf16[256,768]{1,0:T(8,128)(2,1)S(1)}, u32[]{:S(2)}) copy-start(bf16[256,768]{1,0:T(8,128)(2,1)S(1)} %get-tuple-element.61) | copy-start | bytes 1179652
  349.2 17.1 %copy-start.9 = (f32[256,768]{1,0:T(8,128)}, f32[256,768]{1,0:T(8,128)S(1)}, u32[]{:S(2)}) copy-start(f32[256,768]{1,0:T(8,128)S(1)} %get-tuple-element.163) | copy-start | bytes 2359300
  349.2 17.1 %copy-start.121 = (f32[256]{0:T(256)}, f32[256]{0:T(256)S(1)}, u32[]{:S(2)}) copy-start(f32[256]{0:T(256)S(1)} %broadcast_multiply_fusion.4) | copy-start | bytes 3076
  349.4 16.8 %copy-start.132 = (f32[256]{0:T(256)}, f32[256]{0:T(256)S(1)}, u32[]{:S(2)}) copy-start(f32[256]{0:T(256)S(1)} %fusion.453) | copy-start | bytes 3076
  349.5 14.5 %slice-start.10 = ((s8[4718592]{0:T(1024)(128)(4,1)}), s8[4194304]{0:T(1024)(128)(4,1)S(1)}, s32[]{:S(2)}) async-start(s8[4718592]{0:T(1024)(128)(4,1)} %bitcast.441), calls=%async_computation.23 | async-start | bytes 8388608
  354.2 9.8 %copy-start.179 = (f32[256,3072]{1,0:T(8,128)}, f32[256,3072]{1,0:T(8,128)S(1)}, u32[]{:S(2)}) copy-start(f32[256,3072]{1,0:T(8,128)S(1)} %fusion.28) | copy-start | bytes 9437188
  354.2 9.8 %slice-start.11 = ((s8[4718592]{0:T(1024)(128)(4,1)}), s8[524288]{0:T(1024)(128)(4,1)S(1)}, s32[]{:S(2)}) async-start(s8[4718592]{0:T(1024)(128)(4,1)} %bitcast.441), calls=%async_computation.24 | async-start | bytes 1048576
  404.4 26.0 %collective-permute-start.2 = (bf16[256,768]{1,0:T(8,128)(2,1)}, bf16[256,768]{1,0:T(8,128)(2,1)}, u32[]{:S(2)}, u32[]{:S(2)}) collective-permute-start(bf16[256,768]{1,0:T(8,128)(2,1)} %add_convert_fusion.13), channel_id=1, source_target_pairs={{16,0},{17,1},{18,2},{19,3},{20,4},{21,5},{22,6},{23,7},{24,8},{25... | collective-permute-start | bytes 1179656 | tf_op jit(solution)/shard_map/ppermute | solution.py:13
  419.0 12.5 %slice-start.6 = ((s8[4718592]{0:T(1024)(128)(4,1)}), s8[4194304]{0:T(1024)(128)(4,1)S(1)}, s32[]{:S(2)}) async-start(s8[4718592]{0:T(1024)(128)(4,1)} %bitcast.437), calls=%async_computation.19 | async-start | bytes 8388608
  431.5 29.8 %copy-start.30 = (bf16[256,768]{1,0:T(8,128)(2,1)}, bf16[256,768]{1,0:T(8,128)(2,1)S(1)}, u32[]{:S(2)}) copy-start(bf16[256,768]{1,0:T(8,128)(2,1)S(1)} %bitcast_select_fusion.1) | copy-start | bytes 1179652
  462.4 5.8 collective-permute-start.3
  464.0 13.7 %slice-start.14 = ((s8[4718592]{0:T(1024)(128)(4,1)}), s8[524288]{0:T(1024)(128)(4,1)S(1)}, s32[]{:S(2)}) async-start(s8[4718592]{0:T(1024)(128)(4,1)} %bitcast.445), calls=%async_computation.27 | async-start | bytes 1048576
  468.3 11.9 %copy-start.36 = (bf16[256,768]{1,0:T(8,128)(2,1)}, bf16[256,768]{1,0:T(8,128)(2,1)S(1)}, u32[]{:S(2)}) copy-start(bf16[256,768]{1,0:T(8,128)(2,1)S(1)} %bitcast_select_fusion) | copy-start | bytes 1179652
  468.3 9.4 %copy-start.17 = (f32[256,768]{1,0:T(8,128)S(1)}, f32[256,768]{1,0:T(8,128)}, u32[]{:S(2)}) copy-start(f32[256,768]{1,0:T(8,128)} %copy-done.16) | copy-start | bytes 2359300
  488.8 96.9 %reduce-scatter.5.cloned.1.call-start = ((), (), s32[]{:S(2)}) async-start(), calls=%async_computation.4 | async-start | bytes 4423680 | tf_op jit(solution)/shard_map/reduce_scatter | solution.py:222
  501.9 171.6 %reduce-scatter.9.cloned.1.call-start = ((), (), s32[]{:S(2)}) async-start(), calls=%async_computation.6 | async-start | bytes 5898240 | tf_op jit(solution)/shard_map/reduce_scatter | solution.py:234
  514.0 10.8 %copy-start.31 = (bf16[256,768]{1,0:T(8,128)(2,1)S(1)}, bf16[256,768]{1,0:T(8,128)(2,1)}, u32[]{:S(2)}) copy-start(bf16[256,768]{1,0:T(8,128)(2,1)} %copy-done.30) | copy-start | bytes 1179652
  514.0 247.6 %reduce-scatter.11.cloned.1.call-start = ((), (), s32[]{:S(2)}) async-start(), calls=%async_computation.7 | async-start | bytes 5898240 | tf_op jit(solution)/shard_map/reduce_scatter | solution.py:237
  515.1 9.7 %copy-start.183 = (f32[256,3072]{1,0:T(8,128)S(1)}, f32[256,3072]{1,0:T(8,128)}, u32[]{:S(2)}) copy-start(f32[256,3072]{1,0:T(8,128)} %copy-done.182) | copy-start | bytes 9437188
  524.8 10.0 %copy-start.37 = (bf16[256,768]{1,0:T(8,128)(2,1)S(1)}, bf16[256,768]{1,0:T(8,128)(2,1)}, u32[]{:S(2)}) copy-start(bf16[256,768]{1,0:T(8,128)(2,1)} %copy-done.36) | copy-start | bytes 1179652
  524.9 10.0 %copy-start.181 = (f32[256,3072]{1,0:T(8,128)S(1)}, f32[256,3072]{1,0:T(8,128)}, u32[]{:S(2)}) copy-start(f32[256,3072]{1,0:T(8,128)} %fusion.20) | copy-start | bytes 9437188
  546.6 313.3 %all-reduce.14.cloned.1.call-start = ((), (), s32[]{:S(2)}) async-start(), calls=%async_computation.12 | async-start | bytes 7077888 | tf_op jit(solution)/shard_map/psum | solution.py:244
  556.1 205.5 %copy-start.154 = (f32[256]{0:T(256)}, f32[256]{0:T(256)S(1)}, u32[]{:S(2)}) copy-start(f32[256]{0:T(256)S(1)} %broadcast_multiply_fusion.6) | copy-start | bytes 3076
  557.2 204.5 %copy-start.40 = (f32[256,768]{1,0:T(8,128)S(1)}, f32[256,768]{1,0:T(8,128)}, u32[]{:S(2)}) copy-start(f32[256,768]{1,0:T(8,128)} %copy-done.39) | copy-start | bytes 2359300
  761.6 13.7 %copy-start.57 = (bf16[1,256,768]{2,1,0:T(8,128)(2,1)S(1)}, bf16[1,256,768]{2,1,0:T(8,128)(2,1)}, u32[]{:S(2)}) copy-start(bf16[1,256,768]{2,1,0:T(8,128)(2,1)} %select_bitcast_fusion.1) | copy-start | bytes 1179652
  761.6 15.7 %copy-start.8 = (bf16[2,256,768]{2,1,0:T(8,128)(2,1)S(1)}, bf16[2,256,768]{2,1,0:T(8,128)(2,1)}, u32[]{:S(2)}) copy-start(bf16[2,256,768]{2,1,0:T(8,128)(2,1)} %param.11) | copy-start | bytes 2359300
  761.7 15.7 %copy-start.27 = (bf16[256,3,12,64]{0,3,2,1:T(8,128)(2,1)S(1)}, bf16[256,3,12,64]{0,3,2,1:T(8,128)(2,1)}, u32[]{:S(2)}) copy-start(bf16[256,3,12,64]{0,3,2,1:T(8,128)(2,1)} %copy-done.26) | copy-start | bytes 3538948
  761.7 15.7 %copy-start.117 = (f32[256]{0:T(256)S(1)}, f32[256]{0:T(256)}, u32[]{:S(2)}) copy-start(f32[256]{0:T(256)} %copy-done.114) | copy-start | bytes 3076
  777.4 29.5 %copy-start.120 = (f32[256]{0:T(256)S(1)}, f32[256]{0:T(256)}, u32[]{:S(2)}) copy-start(f32[256]{0:T(256)} %copy-done.118) | copy-start | bytes 3076
  777.5 31.1 %copy-start.23 = (f32[256,768]{1,0:T(8,128)S(1)}, f32[256,768]{1,0:T(8,128)}, u32[]{:S(2)}) copy-start(f32[256,768]{1,0:T(8,128)} %copy-done.22) | copy-start | bytes 2359300
  777.5 31.1 %copy-start.38 = (bf16[256,768]{1,0:T(8,128)(2,1)S(1)}, bf16[256,768]{1,0:T(8,128)(2,1)}, u32[]{:S(2)}) copy-start(bf16[256,768]{1,0:T(8,128)(2,1)} %copy-done.36) | copy-start | bytes 1179652
  777.5 31.1 %copy-start.148 = (f32[256]{0:T(256)S(1)}, f32[256]{0:T(256)}, u32[]{:S(2)}) copy-start(f32[256]{0:T(256)} %copy-done.147) | copy-start | bytes 3076
  782.3 26.6 %copy-start.53 = (bf16[1,256,768]{2,1,0:T(8,128)(2,1)S(1)}, bf16[1,256,768]{2,1,0:T(8,128)(2,1)}, u32[]{:S(2)}) copy-start(bf16[1,256,768]{2,1,0:T(8,128)(2,1)} %get-tuple-element.53) | copy-start | bytes 1179652
  (165 other events, 478.4 us)
Sparse Core Ops, SparseCore 0:
  9.7 72.8 all-gather.12
  84.1 29.0 all-gather.14
  114.7 88.5 all-gather.18
  204.7 87.8 all-gather.16
  488.9 29.3 reduce-scatter.6
  520.5 65.0 reduce-scatter.4
  587.9 85.5 reduce-scatter.8
  675.8 85.7 reduce-scatter.10
  765.1 94.8 all-reduce.13
where the time goes:
time: 880 us; the launch traced here: 874 us
  waiting for transfers between devices  508 us (58%)
  matrix products  221 us (25%)
  other arithmetic  45.7 us (5%)
  local copies, waits for them, and re-layouts  37.9 us (4%)
  blocking collectives  35.2 us (4%)
  between operations  18.3 us (2%)
    all_gather x1, waiting for transfers between devices, on_device(): lax.all_gather(shards[6], 'dp', axis=0, tiled=True)  89.3 us
    reduce_scatter x1, waiting for transfers between devices, on_device(): lax.psum_scatter(totals[7].astype(jnp.bfloat16), 'dp', scatter_dimension=...  88.1 us
    all_gather x1, waiting for transfers between devices, on_device(): lax.all_gather(shards[7], 'dp', axis=0, tiled=True)  88 us
    reduce_scatter x1, waiting for transfers between devices, on_device(): lax.psum_scatter(totals[6].astype(jnp.bfloat16), 'dp', scatter_dimension=...  87.9 us
    dot_general x12, matrix products, inner(): lax.dot_general(left, right, (((0,), (0,)), ((), ())), preferred_element_...  59.4 us
    all_gather x1, waiting for transfers between devices, on_device(): lax.all_gather(shards[2], 'dp', axis=0, tiled=True)  53.3 us
    psum x1, waiting for transfers between devices, on_device(): lax.psum(rows[2].astype(jnp.bfloat16), 'group').astype(jnp.float32)  50.1 us
    dot_general x12, matrix products, times_transposed(): lax.dot_general(left, weight, (((1,), (1,)), ((), ())), preferred_element...  46.6 us
  transfers between devices with their start and end apart: 13, of which 10 were waited for; matrix products, arithmetic and copies ran while one was open for 15% of the time, Pallas kernels for 0%

commit v1 on v0

--- a/solution.py
+++ b/solution.py
@@ -1,3 +1,4 @@
+import functools
 import jax
 import jax.numpy as jnp
 from jax import lax
@@ -5,6 +6,25 @@
 
 HEAD_DIM = 64
 masked_score = -1000000000.0
+
+
+def frame_tell(xin, shard_axis, out_dim):
+    n_axis = lax.axis_size(shard_axis)
+    by_place = [xin]
+    for j0 in range(1, n_axis):
+        by_place.append(
+            lax.ppermute(
+                by_place[j0 - 1],
+                shard_axis,
+                [(dev_j, (dev_j - 1) % n_axis) for dev_j in range(n_axis)],
+            )
+        )
+    r1 = jnp.concatenate(by_place, axis=out_dim)
+    all_values = jnp.roll(r1, lax.axis_index(shard_axis) * xin.shape[out_dim], axis=out_dim)
+    return all_values
+
+
+bind_grid = functools.partial(frame_tell, shard_axis="dp", out_dim=0)
 
 
 def from_behind(block, axis, distance):
@@ -175,7 +195,7 @@
         lax.all_gather(shards[4], "dp", axis=0, tiled=True),
         lax.all_gather(shards[5], "dp", axis=0, tiled=True),
         lax.all_gather(shards[6], "dp", axis=0, tiled=True),
-        lax.all_gather(shards[7], "dp", axis=0, tiled=True),
+        bind_grid(shards[7]),
     )
     tables = [rope_tables(lengths[m, 0], tok) for m in range(micro)]
     received = jnp.zeros((tok, width), jnp.bfloat16)

time: 880 us -> 854 us (0.970)
  waiting for transfers between devices: 508 us -> 410 us
  blocking collectives: 35.2 us -> 59.5 us
  local copies, waits for them, and re-layouts: 37.9 us -> 54.9 us
  other arithmetic: 45.7 us -> 57.8 us
  starting transfers between devices: 8.44 us -> 17.4 us
    ppermute x0 -> x3, waiting for transfers between devices: none -> 100 us  [frame_tell(): lax.ppermute(by_place[j0 - 1], shard_axis, [(dev_j, (dev_j - 1) % n_axis)...]
    all_gather x1 -> x0, waiting for transfers between devices: 88 us -> none  [on_device(): lax.all_gather(shards[7], 'dp', axis=0, tiled=True)]
    all_gather x1, waiting for transfers between devices: 53.3 us -> 0.01 us  [on_device(): lax.all_gather(shards[2], 'dp', axis=0, tiled=True)]
    all_gather x1, waiting for transfers between devices: 89.3 us -> 58.2 us  [on_device(): lax.all_gather(shards[6], 'dp', axis=0, tiled=True)]
    unnamed x2, blocking collectives: 25 us -> 49.2 us
    all_gather x1, waiting for transfers between devices: 18.6 us -> 0.02 us  [on_device(): lax.all_gather(shards[3], 'dp', axis=0, tiled=True)]
    unnamed x413 -> x406, local copies, waits for them, and re-layouts: 26.1 us -> 40.5 us
  transfers between devices with their start and end apart: 13 -> 15, of which waited for: 10 -> 9; matrix products, arithmetic and copies ran while one was open for 15% -> 19% of each run, Pallas kernels for 0% -> 0%
where the time goes in v1:
time: 854 us; the launch traced here: 847 us
  waiting for transfers between devices  410 us (48%)
  matrix products  229 us (27%)
  blocking collectives  59.5 us (7%)
  other arithmetic  57.8 us (7%)
  local copies, waits for them, and re-layouts  54.9 us (6%)
  between operations  18.3 us (2%)
  starting transfers between devices  17.4 us (2%)
    ppermute x3, waiting for transfers between devices, frame_tell(): lax.ppermute(by_place[j0 - 1], shard_axis, [(dev_j, (dev_j - 1) % n_axis)...  100 us
    reduce_scatter x1, waiting for transfers between devices, on_device(): lax.psum_scatter(totals[7].astype(jnp.bfloat16), 'dp', scatter_dimension=...  88.1 us
    reduce_scatter x1, waiting for transfers between devices, on_device(): lax.psum_scatter(totals[6].astype(jnp.bfloat16), 'dp', scatter_dimension=...  87.7 us
    dot_general x12, matrix products, inner(): lax.dot_general(left, right, (((0,), (0,)), ((), ())), preferred_element_...  63.3 us
    all_gather x1, waiting for transfers between devices, on_device(): lax.all_gather(shards[6], 'dp', axis=0, tiled=True)  58.2 us
    dot_general x12, matrix products, times_transposed(): lax.dot_general(left, weight, (((1,), (1,)), ((), ())), preferred_element...  51.7 us
    psum x1, waiting for transfers between devices, on_device(): lax.psum(rows[2].astype(jnp.bfloat16), 'group').astype(jnp.float32)  49.8 us
    unnamed x2, blocking collectives  49.2 us
  transfers between devices with their start and end apart: 15, of which 9 were waited for; matrix products, arithmetic and copies ran while one was open for 19% of the time, Pallas kernels for 0%

profile of v1, /device:TPU:0, one launch (start us, length us, event | category | flops | bytes accessed | tf_op | source)
XLA Modules:
  0.0 847.0 jit_solution(6205240477779963054)
XLA Ops:
  8.8 5.1 collective-permute-start
  15.7 53.1 %collective-permute-done = bf16[768,768]{1,0:T(8,128)(2,1)S(1)} collective-permute-done((bf16[768,768]{1,0:T(8,128)(2,1)}, bf16[768,768]{1,0:T(8,128)(2,1)S(1)}, u32[]{:S(2)}, u32[]{:S(2)}) %collective-permute-start) | collective-permute-done | bytes 1179680 | tf_op jit(solution)/shard_map/ppermute | solution.py:16
  73.1 47.1 %collective-permute-done.1 = bf16[768,768]{1,0:T(8,128)(2,1)S(1)} collective-permute-done((bf16[768,768]{1,0:T(8,128)(2,1)S(1)}, bf16[768,768]{1,0:T(8,128)(2,1)S(1)}, u32[]{:S(2)}, u32[]{:S(2)}) %collective-permute-start.1) | collective-permute-done | bytes 1179680 | tf_op jit(solution)/shard_map/ppermute | solution.py:16
  120.2 3.1 collective-permute-start.2
  131.2 38.2 %all-reduce.9 = (bf16[768]{0:T(1024)(128)(2,1)}, bf16[768]{0:T(1024)(128)(2,1)}, bf16[768]{0:T(1024)(128)(2,1)}, bf16[768]{0:T(1024)(128)(2,1)}) all-reduce(bf16[768]{0:T(1024)(128)(2,1)S(1)} %dynamic-update-slice.1, bf16[768]{0:T(1024)(128)(2,1)S(1)} %dynamic-update-slice, ...), channel_id=3, replica_groups=mesh['section'=2,'group'=4,'dp'=4] {'dp'}, use_global_device_ids=true, to_apply=%add.1 | all-reduce | flops 3072 | bytes 12288
  178.7 2.5 constant_dynamic-update-slice_fusion.4
  186.9 5.9 copy.96
  192.8 3.3 fusion.350
  201.4 58.2 %all-gather.15.cloned.1.call-done = bf16[1,768,3072]{2,1,0:T(8,128)(2,1)} async-done(((bf16[1,192,3072]{2,1,0:T(8,128)(2,1)}), bf16[1,768,3072]{2,1,0:T(8,128)(2,1)}) %all-gather.15.cloned.1.call-update) | async-done | bytes 4718608 | tf_op jit(solution)/shard_map/all_gather | solution.py:197
  259.6 13.2 %fusion.262 = bf16[256,768]{1,0:T(8,128)(2,1)S(1)} fusion(f32[256,768]{1,0:T(8,128)S(1)} %get-tuple-element.155, bf16[6144,768]{1,0:T(8,128)(2,1)} %constant_dynamic-update-slice_fusion, s32[]{:T(128)S(6)} %select_n.187, bf16[1,768,3072]{2,1,0:T(8,128)(2,1)} %all-gather.15.cloned.1.call-done, f32[768]{0:T(1024)S(1)} %convert_element_type.462, ...), kind=kOutput, calls=%fused_computation.348 | convolution fusion | flops 2468413440 | bytes 11413508 | tf_op jit(solution)/shard_map/dot_general | solution.py:112
  276.4 3.7 fusion.36
  285.9 13.2 %fusion.257 = bf16[256,768]{1,0:T(8,128)(2,1)S(1)} fusion(f32[256,768]{1,0:T(8,128)S(1)} %get-tuple-element.159, bf16[6144,768]{1,0:T(8,128)(2,1)} %constant_dynamic-update-slice_fusion, s32[]{:T(128)S(6)} %select_n.187, bf16[1,768,3072]{2,1,0:T(8,128)(2,1)} %all-gather.15.cloned.1.call-done, f32[768]{0:T(1024)S(1)} %convert_element_type.462, ...), kind=kOutput, calls=%fused_computation.347 | convolution fusion | flops 2468413440 | bytes 11413508 | tf_op jit(solution)/shard_map/dot_general | solution.py:112
  299.1 3.4 collective-permute-start.4
  310.1 4.6 fusion.597
  314.7 2.5 convolution_convert_fusion.8
  318.1 3.9 fusion.16
  322.1 11.9 %add_convert_fusion.5 = bf16[256,3072]{1,0:T(8,128)(2,1)S(1)} fusion(f32[256,3072]{1,0:T(8,128)S(1)} %fusion.16, bf16[6144,768]{1,0:T(8,128)(2,1)} %constant_dynamic-update-slice_fusion, s32[]{:T(128)S(6)} %select_n.187, bf16[2,256,768]{2,1,0:T(8,128)(2,1)S(1)} %copy-done.45, pred[]{:T(512)S(6)} %eq.72), kind=kOutput, calls=%fused_computation.100 | convolution fusion | flops 1264779264 | bytes 9830405 | tf_op jit(solution)/shard_map/dot_general | solution.py:72
  341.5 2.7 fusion.267
  362.0 4.6 fusion.601
  366.6 2.5 convolution_convert_fusion.5
  378.5 4.6 fusion.603
  383.1 2.6 convolution_convert_fusion.2
  387.4 3.8 fusion.12
  391.4 3.1 fusion.8
  394.5 4.3 fusion.580
  399.9 10.9 %add_convert_fusion.4 = bf16[256,3072]{1,0:T(8,128)(2,1)S(1)} fusion(f32[256,3072]{1,0:T(8,128)S(1)} %fusion.12, bf16[256,768]{1,0:T(8,128)(2,1)S(1)} %bitcast_select_fusion.1, bf16[6144,768]{1,0:T(8,128)(2,1)} %constant_dynamic-update-slice_fusion, s32[]{:T(128)S(6)} %select_n.187), kind=kOutput, calls=%fused_computation.83 | convolution fusion | flops 1264582656 | bytes 9830404 | tf_op jit(solution)/shard_map/dot_general | solution.py:72
  418.3 2.7 fusion.268
  434.3 4.1 fusion.578
  438.5 10.7 %add_convert_fusion.3 = bf16[256,3072]{1,0:T(8,128)(2,1)S(1)} fusion(f32[256,3072]{1,0:T(8,128)S(1)} %copy-done.179, bf16[256,768]{1,0:T(8,128)(2,1)S(1)} %bitcast_select_fusion, bf16[6144,768]{1,0:T(8,128)(2,1)} %constant_dynamic-update-slice_fusion, s32[]{:T(128)S(6)} %select_n.187), kind=kOutput, calls=%fused_computation.66 | convolution fusion | flops 1264582656 | bytes 9830404 | tf_op jit(solution)/shard_map/dot_general | solution.py:72
  454.3 5.3 multiply_reduce_fusion
  461.5 3.5 multiply_convert_fusion.3
  471.3 3.3 add_convert_fusion.2
  475.8 3.1 fusion.577
  479.0 5.1 fusion.579
  484.1 6.5 add_convert_fusion.1
  491.8 9.7 %fusion.112 = f32[3072,768]{1,0:T(8,128)S(1)} fusion(f32[256,3072]{1,0:T(8,128)} %copy-done.178, bf16[2,256,768]{2,1,0:T(8,128)(2,1)S(1)} %copy-done.49, pred[]{:T(512)S(6)} %eq.72), kind=kOutput, calls=%fused_computation.191 | convolution fusion | flops 1259274240 | bytes 12976129 | tf_op jit(solution)/shard_map/dot_general | solution.py:66
  501.5 9.9 %fusion.113 = f32[3072,768]{1,0:T(8,128)} fusion(bf16[256,768]{1,0:T(8,128)(2,1)S(1)} %bitcast_select_fusion.1, f32[256,3072]{1,0:T(8,128)S(1)} %copy-done.182), kind=kOutput, calls=%fused_computation.192 | convolution fusion | flops 1259077632 | bytes 12976128 | tf_op jit(solution)/shard_map/dot_general | solution.py:66
  511.5 11.8 %add_convert_fusion = bf16[3072,768]{1,0:T(8,128)(2,1)} fusion(f32[3072,768]{1,0:T(8,128)} %fusion.113, f32[3072,768]{1,0:T(8,128)S(1)} %fusion.112, bf16[256,768]{1,0:T(8,128)(2,1)S(1)} %copy-done.37, f32[]{:T(128)S(6)} %select_n.213, f32[]{:T(128)S(6)} %select_n.212, f32[256,3072]{1,0:T(8,128)S(1)} %copy-done.180), kind=kOutput, calls=%fused_computation.6 | convolution fusion | flops 1270874112 | bytes 27131912 | tf_op jit(solution)/shard_map/dot_general | solution.py:66
  526.0 3.8 fusion.34
  535.2 22.9 %reduce-scatter.5.cloned.1.call-done = bf16[192,2304]{1,0:T(8,128)(2,1)} async-done(((bf16[768,2304]{1,0:T(8,128)(2,1)}), bf16[192,2304]{1,0:T(8,128)(2,1)}) %reduce-scatter.5.cloned.1.call-update) | async-done | bytes 884752 | tf_op jit(solution)/shard_map/reduce_scatter | solution.py:242
  558.1 87.7 %reduce-scatter.9.cloned.1.call-done = bf16[192,3072]{1,0:T(8,128)(2,1)} async-done(((bf16[768,3072]{1,0:T(8,128)(2,1)}), bf16[192,3072]{1,0:T(8,128)(2,1)}) %reduce-scatter.9.cloned.1.call-update) | async-done | bytes 1179664 | tf_op jit(solution)/shard_map/reduce_scatter | solution.py:254
  645.8 88.1 %reduce-scatter.11.cloned.1.call-done = bf16[768,768]{1,0:T(8,128)(2,1)} async-done(((bf16[3072,768]{1,0:T(8,128)(2,1)}), bf16[768,768]{1,0:T(8,128)(2,1)}) %reduce-scatter.11.cloned.1.call-update) | async-done | bytes 1179664 | tf_op jit(solution)/shard_map/reduce_scatter | solution.py:257
  734.0 14.1 %fusion.299 = bf16[1,256,768]{2,1,0:T(8,128)(2,1)} fusion(bf16[256,768]{1,0:T(8,128)(2,1)} %copy-done.89, f32[256,768]{1,0:T(8,128)S(1)} %copy-done.40, bf16[6144,768]{1,0:T(8,128)(2,1)} %constant_dynamic-update-slice_fusion, s32[]{:T(128)S(6)} %select_n.187, bf16[1,768,3072]{2,1,0:T(8,128)(2,1)} %all-gather.15.cloned.1.call-done, ...), kind=kOutput, calls=%fused_computation.375 | convolution fusion | flops 2468610048 | bytes 11806725 | tf_op jit(solution)/shard_map/dot_general | solution.py:112
  750.1 4.8 multiply_reduce_fusion.6
  755.1 11.1 %all-reduce.8 = (bf16[768]{0:T(1024)(128)(2,1)S(1)}, bf16[768]{0:T(1024)(128)(2,1)S(1)}, bf16[768]{0:T(1024)(128)(2,1)S(1)}, bf16[768]{0:T(1024)(128)(2,1)S(1)}) all-reduce(bf16[768]{0:T(1024)(128)(2,1)S(1)} %add_convert_fusion.46, ...), channel_id=9, replica_groups=mesh['section'=2,'group'=4,'dp'=4] {'dp'}, use_global_device_ids=true, to_apply=%region_60.61.clone | all-reduce | flops 3072 | bytes 12288
  766.5 10.3 %all-reduce.10 = (bf16[1,192]{1,0:T(2,128)(2,1)S(1)}, bf16[1,192]{1,0:T(2,128)(2,1)S(1)}, bf16[1,192]{1,0:T(2,128)(2,1)S(1)}, bf16[1,192]{1,0:T(2,128)(2,1)S(1)}) all-reduce(bf16[1,192]{1,0:T(2,128)(2,1)S(1)} %broadcast_in_dim.143, ...), channel_id=1, replica_groups=mesh['section'=2,'group'=4,'dp'=4] {'group'}, use_global_device_ids=true, to_apply=%region_61.62 | all-reduce | flops 768 | bytes 3072 | tf_op jit(solution)/shard_map/psum | solution.py:262
  782.5 49.8 %all-reduce.14.cloned.1.call-done = (bf16[1,192,2304]{2,1,0:T(8,128)(2,1)}, bf16[1,192,768]{2,1,0:T(8,128)(2,1)}, bf16[1,192,3072]{2,1,0:T(8,128)(2,1)}, bf16[1,768,768]{2,1,0:T(8,128)(2,1)}) async-done(((bf16[1,192,2304]{2,1,0:T(8,128)(2,1)}, bf16[1,192,768]{2,1,0:T(8,128)(2,1)}, bf16[1,192,3072]{2,1,0:T(8,128)(2,1)}, bf16[1,768,768]{2,1,0:T(8,128)(2,1)}), (bf16[1,192,2304]{2,1,0:T(8,128)(2,1)}, ...) | async-done | bytes 3538960 | tf_op jit(solution)/shard_map/psum | solution.py:264
  832.3 2.6 broadcast_in_dim.148
  (610 shorter events, 145.9 us)
Async XLA Ops:
  7.2 119.5 %copy-start.173 = (u32[32]{0:T(128)S(1)}, u32[32]{0:T(128)}, u32[]{:S(2)}) copy-start(u32[32]{0:T(128)} %constant.167) | copy-start | bytes 388
  7.2 168.3 %copy-start.29 = (bf16[1,768,768]{2,1,0:T(8,128)(2,1)S(1)}, bf16[1,768,768]{2,1,0:T(8,128)(2,1)}, u32[]{:S(2)}) copy-start(bf16[1,768,768]{2,1,0:T(8,128)(2,1)} %param.21) | copy-start | bytes 3538948
  7.2 116.6 %copy-start.174 = (bf16[1,192]{1,0:T(2,128)(2,1)S(1)}, bf16[1,192]{1,0:T(2,128)(2,1)}, u32[]{:S(2)}) copy-start(bf16[1,192]{1,0:T(2,128)(2,1)} %param.15) | copy-start | bytes 1156
  7.2 117.2 %copy-start.175 = (bf16[1,192]{1,0:T(2,128)(2,1)S(1)}, bf16[1,192]{1,0:T(2,128)(2,1)}, u32[]{:S(2)}) copy-start(bf16[1,192]{1,0:T(2,128)(2,1)} %param.14) | copy-start | bytes 1156
  7.2 117.7 %copy-start.176 = (bf16[1,192]{1,0:T(2,128)(2,1)S(1)}, bf16[1,192]{1,0:T(2,128)(2,1)}, u32[]{:S(2)}) copy-start(bf16[1,192]{1,0:T(2,128)(2,1)} %param.19) | copy-start | bytes 1156
  7.2 179.7 %all-gather.11.cloned.1.call-start = ((), (), s32[]{:S(2)}) async-start(), calls=%async_computation.8 | async-start | bytes 4423680 | tf_op jit(solution)/shard_map/all_gather | solution.py:193
  8.0 191.3 %all-gather.13.cloned.1.call-start = ((), (), s32[]{:S(2)}) async-start(), calls=%async_computation.9 | async-start | bytes 1474560 | tf_op jit(solution)/shard_map/all_gather | solution.py:194
  8.7 250.9 %all-gather.15.cloned.1.call-start = ((), (), s32[]{:S(2)}) async-start(), calls=%async_computation.10 | async-start | bytes 5898240 | tf_op jit(solution)/shard_map/all_gather | solution.py:197
  8.8 60.1 %collective-permute-start = (bf16[768,768]{1,0:T(8,128)(2,1)}, bf16[768,768]{1,0:T(8,128)(2,1)S(1)}, u32[]{:S(2)}, u32[]{:S(2)}) collective-permute-start(bf16[768,768]{1,0:T(8,128)(2,1)} %bitcast.368), channel_id=1, source_target_pairs={{0,3},{1,0},{2,1},{3,2},{4,7},{5,4},{6,5},{7,6},{8,11},{9,8},{10,9... | collective-permute-start | bytes 3538952 | tf_op jit(solution)/shard_map/ppermute | solution.py:16
  13.9 521.4 %reduce-scatter.7.cloned.1.call-start = ((), (), s32[]{:S(2)}) async-start(), calls=%async_computation.5 | async-start | bytes 1474560 | tf_op jit(solution)/shard_map/reduce_scatter | solution.py:245
  15.1 53.9 %copy-start.134 = (s32[256]{0:T(256)}, s32[256]{0:T(256)S(1)}, u32[]{:S(2)}) copy-start(s32[256]{0:T(256)S(1)} %fusion.436) | copy-start | bytes 3076
  68.8 51.3 %collective-permute-start.1 = (bf16[768,768]{1,0:T(8,128)(2,1)S(1)}, bf16[768,768]{1,0:T(8,128)(2,1)S(1)}, u32[]{:S(2)}, u32[]{:S(2)}) collective-permute-start(bf16[768,768]{1,0:T(8,128)(2,1)S(1)} %collective-permute-done), channel_id=1, source_target_pairs={{0,3},{1,0},{2,1},{3,2},{4,7},{5,4},{6,5},{7,6},{8,11},{9,8},{10,9... | collective-permute-start | bytes 3538952 | tf_op jit(solution)/shard_map/ppermute | solution.py:16
  70.7 49.5 %copy-start.139 = (f32[256]{0:T(256)}, f32[256]{0:T(256)S(1)}, u32[]{:S(2)}) copy-start(f32[256]{0:T(256)S(1)} %broadcast_multiply_fusion.11) | copy-start | bytes 3076
  120.2 58.5 %collective-permute-start.2 = (bf16[768,768]{1,0:T(8,128)(2,1)S(1)}, bf16[768,768]{1,0:T(8,128)(2,1)}, u32[]{:S(2)}, u32[]{:S(2)}) collective-permute-start(bf16[768,768]{1,0:T(8,128)(2,1)S(1)} %collective-permute-done.1), channel_id=1, source_target_pairs={{0,3},{1,0},{2,1},{3,2},{4,7},{5,4},{6,5},{7,6},{8,11},{9,8},{10,9... | collective-permute-start | bytes 3538952 | tf_op jit(solution)/shard_map/ppermute | solution.py:16
  272.8 3.2 collective-permute-start.3
  299.1 3.8 collective-permute-start.4
  303.8 90.7 %copy-start.5 = (bf16[256,768]{1,0:T(8,128)(2,1)}, bf16[256,768]{1,0:T(8,128)(2,1)S(1)}, u32[]{:S(2)}) copy-start(bf16[256,768]{1,0:T(8,128)(2,1)S(1)} %get-tuple-element.63) | copy-start | bytes 1179652
  317.8 18.4 %copy-start.8 = (f32[256,768]{1,0:T(8,128)}, f32[256,768]{1,0:T(8,128)S(1)}, u32[]{:S(2)}) copy-start(f32[256,768]{1,0:T(8,128)S(1)} %get-tuple-element.163) | copy-start | bytes 2359300
  317.8 18.4 %copy-start.121 = (f32[256]{0:T(256)}, f32[256]{0:T(256)S(1)}, u32[]{:S(2)}) copy-start(f32[256]{0:T(256)S(1)} %broadcast_multiply_fusion.4) | copy-start | bytes 3076
  318.0 18.1 %copy-start.131 = (f32[256]{0:T(256)}, f32[256]{0:T(256)S(1)}, u32[]{:S(2)}) copy-start(f32[256]{0:T(256)S(1)} %fusion.438) | copy-start | bytes 3076
  318.1 15.9 %slice-start.4 = ((s8[4718592]{0:T(1024)(128)(4,1)}), s8[4194304]{0:T(1024)(128)(4,1)S(1)}, s32[]{:S(2)}) async-start(s8[4718592]{0:T(1024)(128)(4,1)} %bitcast.395), calls=%async_computation.16 | async-start | bytes 8388608
  322.0 11.9 %copy-start.178 = (f32[256,3072]{1,0:T(8,128)}, f32[256,3072]{1,0:T(8,128)S(1)}, u32[]{:S(2)}) copy-start(f32[256,3072]{1,0:T(8,128)S(1)} %fusion.16) | copy-start | bytes 9437188
  322.1 11.9 %slice-start.5 = ((s8[4718592]{0:T(1024)(128)(4,1)}), s8[524288]{0:T(1024)(128)(4,1)S(1)}, s32[]{:S(2)}) async-start(s8[4718592]{0:T(1024)(128)(4,1)} %bitcast.395), calls=%async_computation.17 | async-start | bytes 1048576
  372.8 26.0 %collective-permute-start.5 = (bf16[256,768]{1,0:T(8,128)(2,1)}, bf16[256,768]{1,0:T(8,128)(2,1)}, u32[]{:S(2)}, u32[]{:S(2)}) collective-permute-start(bf16[256,768]{1,0:T(8,128)(2,1)} %add_convert_fusion.13), channel_id=1, source_target_pairs={{16,0},{17,1},{18,2},{19,3},{20,4},{21,5},{22,6},{23,7},{24,8},{25... | collective-permute-start | bytes 1179656 | tf_op jit(solution)/shard_map/ppermute | solution.py:33
  383.1 8.1 slice-start.6
  391.3 8.5 %copy-start.181 = (f32[256,3072]{1,0:T(8,128)}, f32[256,3072]{1,0:T(8,128)S(1)}, u32[]{:S(2)}) copy-start(f32[256,3072]{1,0:T(8,128)S(1)} %fusion.12) | copy-start | bytes 9437188
  432.5 5.9 collective-permute-start.6
  434.3 14.9 %slice-start.8 = ((s8[4718592]{0:T(1024)(128)(4,1)}), s8[4194304]{0:T(1024)(128)(4,1)S(1)}, s32[]{:S(2)}) async-start(s8[4718592]{0:T(1024)(128)(4,1)} %bitcast.399), calls=%async_computation.20 | async-start | bytes 8388608
  438.5 13.3 %copy-start.36 = (bf16[256,768]{1,0:T(8,128)(2,1)}, bf16[256,768]{1,0:T(8,128)(2,1)S(1)}, u32[]{:S(2)}) copy-start(bf16[256,768]{1,0:T(8,128)(2,1)S(1)} %bitcast_select_fusion) | copy-start | bytes 1179652
  438.5 10.7 %copy-start.16 = (f32[256,768]{1,0:T(8,128)S(1)}, f32[256,768]{1,0:T(8,128)}, u32[]{:S(2)}) copy-start(f32[256,768]{1,0:T(8,128)} %copy-done.15) | copy-start | bytes 2359300
  438.5 10.7 %copy-start.129 = (f32[256]{0:T(256)S(1)}, f32[256]{0:T(256)}, u32[]{:S(2)}) copy-start(f32[256]{0:T(256)} %copy-done.128) | copy-start | bytes 3076
  438.5 10.7 %copy-start.137 = (f32[256]{0:T(256)S(1)}, f32[256]{0:T(256)}, u32[]{:S(2)}) copy-start(f32[256]{0:T(256)} %copy-done.136) | copy-start | bytes 3076
  438.5 10.7 %slice-start.9 = ((s8[4718592]{0:T(1024)(128)(4,1)}), s8[524288]{0:T(1024)(128)(4,1)S(1)}, s32[]{:S(2)}) async-start(s8[4718592]{0:T(1024)(128)(4,1)} %bitcast.399), calls=%async_computation.21 | async-start | bytes 1048576
  461.2 96.9 %reduce-scatter.5.cloned.1.call-start = ((), (), s32[]{:S(2)}) async-start(), calls=%async_computation.4 | async-start | bytes 4423680 | tf_op jit(solution)/shard_map/reduce_scatter | solution.py:242
  474.6 171.2 %reduce-scatter.9.cloned.1.call-start = ((), (), s32[]{:S(2)}) async-start(), calls=%async_computation.6 | async-start | bytes 5898240 | tf_op jit(solution)/shard_map/reduce_scatter | solution.py:254
  490.7 243.2 %reduce-scatter.11.cloned.1.call-start = ((), (), s32[]{:S(2)}) async-start(), calls=%async_computation.7 | async-start | bytes 5898240 | tf_op jit(solution)/shard_map/reduce_scatter | solution.py:257
  491.8 9.7 %copy-start.182 = (f32[256,3072]{1,0:T(8,128)S(1)}, f32[256,3072]{1,0:T(8,128)}, u32[]{:S(2)}) copy-start(f32[256,3072]{1,0:T(8,128)} %copy-done.181) | copy-start | bytes 9437188
  501.5 9.9 %copy-start.37 = (bf16[256,768]{1,0:T(8,128)(2,1)S(1)}, bf16[256,768]{1,0:T(8,128)(2,1)}, u32[]{:S(2)}) copy-start(bf16[256,768]{1,0:T(8,128)(2,1)} %copy-done.36) | copy-start | bytes 1179652
  501.5 9.9 %copy-start.180 = (f32[256,3072]{1,0:T(8,128)S(1)}, f32[256,3072]{1,0:T(8,128)}, u32[]{:S(2)}) copy-start(f32[256,3072]{1,0:T(8,128)} %fusion.8) | copy-start | bytes 9437188
  523.3 309.0 %all-reduce.14.cloned.1.call-start = ((), (), s32[]{:S(2)}) async-start(), calls=%async_computation.11 | async-start | bytes 7077888 | tf_op jit(solution)/shard_map/psum | solution.py:264
  534.7 199.3 %copy-start.40 = (f32[256,768]{1,0:T(8,128)S(1)}, f32[256,768]{1,0:T(8,128)}, u32[]{:S(2)}) copy-start(f32[256,768]{1,0:T(8,128)} %copy-done.39) | copy-start | bytes 2359300
  734.0 16.0 %copy-start.28 = (bf16[256,3,12,64]{0,3,2,1:T(8,128)(2,1)S(1)}, bf16[256,3,12,64]{0,3,2,1:T(8,128)(2,1)}, u32[]{:S(2)}) copy-start(bf16[256,3,12,64]{0,3,2,1:T(8,128)(2,1)} %copy-done.27) | copy-start | bytes 3538948
  734.0 16.0 %copy-start.117 = (f32[256]{0:T(256)S(1)}, f32[256]{0:T(256)}, u32[]{:S(2)}) copy-start(f32[256]{0:T(256)} %copy-done.114) | copy-start | bytes 3076
  750.1 29.6 %copy-start.120 = (f32[256]{0:T(256)S(1)}, f32[256]{0:T(256)}, u32[]{:S(2)}) copy-start(f32[256]{0:T(256)} %copy-done.118) | copy-start | bytes 3076
  750.1 31.1 %copy-start.23 = (f32[256,768]{1,0:T(8,128)S(1)}, f32[256,768]{1,0:T(8,128)}, u32[]{:S(2)}) copy-start(f32[256,768]{1,0:T(8,128)} %copy-done.22) | copy-start | bytes 2359300
  750.1 31.1 %copy-start.38 = (bf16[256,768]{1,0:T(8,128)(2,1)S(1)}, bf16[256,768]{1,0:T(8,128)(2,1)}, u32[]{:S(2)}) copy-start(bf16[256,768]{1,0:T(8,128)(2,1)} %copy-done.36) | copy-start | bytes 1179652
  750.1 31.1 %copy-start.150 = (f32[256]{0:T(256)S(1)}, f32[256]{0:T(256)}, u32[]{:S(2)}) copy-start(f32[256]{0:T(256)} %copy-done.149) | copy-start | bytes 3076
  754.9 26.6 %copy-start.54 = (bf16[1,256,768]{2,1,0:T(8,128)(2,1)S(1)}, bf16[1,256,768]{2,1,0:T(8,128)(2,1)}, u32[]{:S(2)}) copy-start(bf16[1,256,768]{2,1,0:T(8,128)(2,1)} %get-tuple-element.53) | copy-start | bytes 1179652
  (160 other events, 422.4 us)
Sparse Core Ops, SparseCore 0:
  9.6 112.8 all-gather.10
  124.1 42.2 all-gather.12
  167.9 91.6 all-gather.14
  461.3 29.4 reduce-scatter.6
  493.0 65.0 reduce-scatter.4
  560.2 85.5 reduce-scatter.8
  648.1 85.7 reduce-scatter.10
  737.4 94.8 all-reduce.13
